TPU v7x, 32 devices: a whole 2x2x4 slice. The times are simulated.
32 devices in a mesh: ia: 8 (over y, x, core), ja: 4 (over z).
Axes of the slice: x: 2, y: 2, z: 4, core: 2. Of those that a mesh axis runs over, the one named last changes fastest.
Arguments:
- slabs: bfloat16 [32, 512, 512], P(('ia', 'ja')), may hold values from -1.1953125 to 1.1953125
- pno_coef: bfloat16 [512, 256, 128], P(('ia', 'ja')), may hold values from -0.375 to 0.375
- dom_blocks: int32 [512, 2], P(('ia', 'ja')), may hold values from 0 to 3, as said below
- pair_first: int32 [512], P(('ia', 'ja')), may hold values from 0 to 3
- pair_second: int32 [512], P(('ia', 'ja')), may hold values from 0 to 7
- pno_energy: float32 [512, 128], P(('ia', 'ja')), may hold values from 0.3 to 3
- pair_shift: float32 [512], P(('ia', 'ja')), may hold values from 0.5 to 2
- margin_i: bfloat16 [512, 16, 128, 128], P(('ia', 'ja')), may hold values from -0.5 to 0.5
- margin_j: bfloat16 [512, 16, 128, 128], P(('ia', 'ja')), may hold values from -0.5 to 0.5
- couple_i: float32 [512, 16], P(('ia', 'ja')), may hold values from -0.45 to 0.45
- couple_j: float32 [512, 16], P(('ia', 'ja')), may hold values from -0.45 to 0.45
- ask_i: int32 [32, 8, 4], P(('ia', 'ja')), may hold values from 0 to 15, as said below
- ask_j: int32 [32, 4, 4], P(('ia', 'ja')), may hold values from 0 to 15, as said below
- link_i: int32 [512, 16], P(('ia', 'ja')), may hold values from 0 to 31, as said below
- link_j: int32 [512, 16], P(('ia', 'ja')), may hold values from 0 to 15, as said below
Outputs:
- amplitudes: float32 [512, 128, 128], P(('ia', 'ja'))
- density: float32 [512, 512], P(('ia', 'ja'))
Inputs may be any that keep to these rules, and one draw needn't show every extreme that they name: `dom_blocks`: the 2 blocks of a pair are distinct. `ask_i`: for each block g and each peer s, the 4 slots are distinct. `ask_j`: for each block g and each peer s, the 4 slots are distinct. `link_i`: within each aligned block of 16 pairs every value is named at least once. `link_j`: within each aligned block of 16 pairs every value is named at least once.
All inputs are finite; a program needn't handle non-finite values.
Results may differ from a plain program's by a relative error of at most 0.0045.
Values may be sent and summed in bfloat16 or wider, within the bound.
A program may use at most 128 MiB of HBM per device.

v0:
```python
import math
import jax
import jax.numpy as jnp
from jax import lax
from jax.sharding import PartitionSpec as P

BLK = 128
ITERS = 2


def coupled(near_blocks, margin_blocks, weights):
    left_side = jnp.einsum(
        "pnab,pnbc->pnac", margin_blocks, near_blocks, preferred_element_type=jnp.float32
    ).astype(jnp.bfloat16)
    product = jnp.einsum(
        "pnac,pndc->pnad", left_side, margin_blocks, preferred_element_type=jnp.float32
    )
    return jnp.sum(weights[:, :, None, None] * product, axis=1)


def body(
    slabs,
    pno_coef,
    dom_blocks,
    pair_first,
    pair_second,
    pno_energy,
    pair_shift,
    margin_i,
    margin_j,
    couple_i,
    couple_j,
    ask_i,
    ask_j,
    link_i,
    link_j,
):
    pair_count = pno_coef.shape[0]
    pno_count = pno_coef.shape[2]
    pao_count = slabs.shape[1]
    aux_count = slabs.shape[2]
    block_count = pao_count // BLK
    domain_count = dom_blocks.shape[1]
    row_peers = lax.axis_size("ia")
    col_peers = lax.axis_size("ja")
    row_slots = ask_i.shape[2]
    col_slots = ask_j.shape[2]
    row_slabs = lax.all_gather(slabs, "ja", axis=0, tiled=True)
    col_slabs = lax.all_gather(slabs, "ia", axis=0, tiled=True)
    rows_first = row_slabs.reshape(-1, BLK, aux_count)[
        pair_first[:, None] * block_count + dom_blocks
    ].reshape(pair_count, -1, aux_count)
    rows_second = col_slabs.reshape(-1, BLK, aux_count)[
        pair_second[:, None] * block_count + dom_blocks
    ].reshape(pair_count, -1, aux_count)
    projected_first = jnp.einsum(
        "pmn,pmq->pnq", pno_coef, rows_first, preferred_element_type=jnp.float32
    ).astype(jnp.bfloat16)
    projected_second = jnp.einsum(
        "pmn,pmq->pnq", pno_coef, rows_second, preferred_element_type=jnp.float32
    ).astype(jnp.bfloat16)
    exchange_ints = jnp.einsum(
        "paq,pbq->pab", projected_first, projected_second, preferred_element_type=jnp.float32
    )
    denominator = pno_energy[:, :, None] + pno_energy[:, None, :] + pair_shift[:, None, None]
    amplitudes = -exchange_ints / denominator
    asked_rows = lax.all_to_all(ask_i, "ia", split_axis=1, concat_axis=0, tiled=True).reshape(
        row_peers, row_slots
    )
    asked_cols = lax.all_to_all(ask_j, "ja", split_axis=1, concat_axis=0, tiled=True).reshape(
        col_peers, col_slots
    )
    for iteration in range(ITERS):
        sent = amplitudes.astype(jnp.bfloat16)
        table_rows = lax.all_to_all(
            sent[asked_rows], "ia", split_axis=0, concat_axis=0, tiled=True
        ).reshape(-1, pno_count, pno_count)
        table_cols = lax.all_to_all(
            sent[asked_cols], "ja", split_axis=0, concat_axis=0, tiled=True
        ).reshape(-1, pno_count, pno_count)
        near_rows = table_rows[link_i]
        near_cols = table_cols[link_j]
        coupling = coupled(near_rows, margin_i, couple_i) + coupled(near_cols, margin_j, couple_j)
        residual = exchange_ints + denominator * amplitudes + coupling
        amplitudes = amplitudes - residual / denominator
    sent = amplitudes.astype(jnp.bfloat16)
    square = (
        jnp.einsum("pab,pcb->pac", sent, sent, preferred_element_type=jnp.float32)
        + jnp.einsum("pba,pbc->pac", sent, sent, preferred_element_type=jnp.float32)
    ).astype(jnp.bfloat16)
    mapped = jnp.einsum(
        "pmn,pnk->pmk", pno_coef, square, preferred_element_type=jnp.float32
    ).astype(jnp.bfloat16)
    mapped_blocks = mapped.reshape(pair_count, domain_count, BLK, pno_count)
    coef_blocks = pno_coef.reshape(pair_count, domain_count, BLK, pno_count)
    domain_density = jnp.einsum(
        "pkrn,plcn->pklrc", mapped_blocks, coef_blocks, preferred_element_type=jnp.float32
    )
    select = (
        dom_blocks[:, :, None] == jnp.arange(block_count, dtype=jnp.int32)[None, None, :]
    ).astype(jnp.float32)
    placement = jnp.einsum("pkg,plh->ghpkl", select, select).reshape(
        block_count * block_count, pair_count * domain_count * domain_count
    )
    stacked = jnp.dot(
        placement,
        domain_density.reshape(pair_count * domain_count * domain_count, BLK * BLK),
        precision=lax.Precision.HIGHEST,
        preferred_element_type=jnp.float32,
    )
    partial_sum = (
        stacked.reshape(block_count, block_count, BLK, BLK)
        .transpose(0, 2, 1, 3)
        .reshape(pao_count, pao_count)
    )
    all_devices = lax.axis_size(("ia", "ja"))
    factor = 1.0 / math.sqrt(pair_count * all_devices)
    owned_rows = pao_count // all_devices
    summed = lax.psum(partial_sum, ("ia", "ja"))
    owned = lax.dynamic_slice_in_dim(
        summed, lax.axis_index(("ia", "ja")) * owned_rows, owned_rows, 0
    )
    return (amplitudes, owned * factor)


def solution(mesh):
    in_specs = (
        P(("ia", "ja"), None, None),
        P(("ia", "ja"), None, None),
        P(("ia", "ja"), None),
        P(("ia", "ja")),
        P(("ia", "ja")),
        P(("ia", "ja"), None),
        P(("ia", "ja")),
        P(("ia", "ja"), None, None, None),
        P(("ia", "ja"), None, None, None),
        P(("ia", "ja"), None),
        P(("ia", "ja"), None),
        P(("ia", "ja"), None, None),
        P(("ia", "ja"), None, None),
        P(("ia", "ja"), None),
        P(("ia", "ja"), None),
    )
    out_specs = (P(("ia", "ja"), None, None), P(("ia", "ja"), None))
    return jax.shard_map(body, mesh=mesh, in_specs=in_specs, out_specs=out_specs, check_vma=False)
```

profile of v0, /device:TPU:0, one launch (start us, length us, event | category | flops | bytes accessed | tf_op | source)
XLA Modules:
  0.0 441.4 jit_solution(10866756121001546754)
XLA Ops:
  7.2 0.0 copy-start
  7.2 0.0 all-gather.3.cloned.1.call-start
  7.2 0.7 all-gather.3.cloned.1.call-update
  7.9 0.0 all-gather.5.cloned.1.call-start
  8.0 0.7 all-gather.5.cloned.1.call-update
  8.7 6.4 %all-to-all-start.2 = ((s32[1,4,4]{2,0,1:T(1,128)}), s32[1,4,4]{2,0,1:T(1,128)S(1)}, u32[]{:S(2)}, u32[]{:S(2)}) async-start(s32[1,4,4]{2,0,1:T(1,128)} %bitcast.108), calls=%async_computation.2 | async-start | bytes 4096 | tf_op jit(solution)/shard_map/all_to_all | solution.py:70
  15.0 0.7 broadcast_multiply_fusion.1
  15.7 0.7 compare_select_fusion.5
  16.4 0.1 copy.50
  16.5 0.1 reshape.149
  16.6 0.1 copy.48
  16.6 0.1 reshape.141
  16.8 1.4 copy.53
  18.1 2.4 all-to-all-done.2
  20.5 3.7 all-to-all-start
  24.3 0.1 reshape.173
  24.3 33.6 %all-gather.3.cloned.1.call-done = bf16[4,512,512]{2,1,0:T(8,128)(2,1)} async-done(((bf16[1,512,512]{2,1,0:T(8,128)(2,1)}), bf16[4,512,512]{2,1,0:T(8,128)(2,1)}) %all-gather.3.cloned.1.call-update) | async-done | bytes 2097168 | tf_op jit(solution)/shard_map/all_gather | solution.py:48
  58.0 4.4 %gather_fusion = bf16[32,128,512]{2,1,0:T(8,128)(2,1)} fusion(bf16[16,128,512]{2,1,0:T(8,128)(2,1)} %bitcast.93, s32[1024]{0:T(1024)S(1)} %pad_clamp_fusion.5), kind=kCustom, calls=%fused_computation | custom fusion | bytes 8388736 | tf_op jit(solution)/shard_map/gather | solution.py:50
  62.4 32.9 %all-gather.5.cloned.1.call-done = bf16[8,512,512]{2,1,0:T(8,128)(2,1)} async-done(((bf16[1,512,512]{2,1,0:T(8,128)(2,1)}), bf16[8,512,512]{2,1,0:T(8,128)(2,1)}) %all-gather.5.cloned.1.call-update) | async-done | bytes 4194320 | tf_op jit(solution)/shard_map/all_gather | solution.py:49
  95.3 5.0 %gather_fusion.1 = bf16[32,128,512]{2,1,0:T(8,128)(2,1)} fusion(bf16[32,128,512]{2,1,0:T(8,128)(2,1)} %bitcast.98, s32[1024]{0:T(1024)S(1)} %pad_clamp_fusion.4), kind=kCustom, calls=%fused_computation.1 | custom fusion | bytes 8388736 | tf_op jit(solution)/shard_map/gather | solution.py:53
  100.3 0.0 copy-start.5
  100.3 0.0 copy-start.6
  100.3 7.5 %fusion.36 = (bf16[16,128,128]{2,1,0:T(8,128)(2,1)S(1)}, f32[16,128,128]{2,1,0:T(8,128)}) fusion(f32[16]{0:T(128)S(1)} %copy-done.8, f32[16,128]{1,0:T(8,128)S(1)} %copy-done.4, bf16[16,256,512]{2,1,0:T(8,128)(2,1)} %bitcast.100, bf16[16,256,128]{2,1,0:T(8,128)(2,1)S(1)} %copy-done, bf16[16,256,512]{2,1,0:T(8,128)(2,1)} %bitcast.99), kind=kOutput, calls=%fused_computation.44 | convolution fusion | flops 1345585152 | bytes 11018304 | tf_op jit(solution)/shard_map/paq,pbq->pab/dot_general | solution.py:62
  107.8 1.4 gather_fusion.4
  109.2 0.0 all-to-all-done
  109.2 4.6 %all-to-all-start.3 = ((bf16[4,4,128,128]{3,2,1,0:T(8,128)(2,1)}), bf16[4,4,128,128]{3,2,1,0:T(8,128)(2,1)S(1)}, u32[]{:S(2)}, u32[]{:S(2)}) async-start(bf16[4,4,128,128]{3,2,1,0:T(8,128)(2,1)} %bitcast.10), calls=%async_computation.3 | async-start | bytes 1048576 | tf_op jit(solution)/shard_map/all_to_all | solution.py:78
  113.8 0.1 reshape.165
  113.9 0.1 reshape.181
  114.0 0.1 copy.54
  114.1 0.1 copy.55
  114.2 0.1 reshape.157
  114.3 1.7 gather_fusion.2
  116.0 12.8 %all-to-all-done.3 = bf16[4,4,128,128]{3,2,1,0:T(8,128)(2,1)S(1)} async-done(((bf16[4,4,128,128]{3,2,1,0:T(8,128)(2,1)}), bf16[4,4,128,128]{3,2,1,0:T(8,128)(2,1)S(1)}, u32[]{:S(2)}, u32[]{:S(2)}) %all-to-all-start.3) | async-done | bytes 524320 | tf_op jit(solution)/shard_map/all_to_all | solution.py:78
  128.7 3.9 all-to-all-start.1
  132.7 0.0 copy-start.9
  132.7 8.6 %gather_fusion.5 = bf16[256,128,128]{2,1,0:T(8,128)(2,1)} fusion(bf16[16,128,128]{2,1,0:T(8,128)(2,1)S(1)} %bitcast.88, s32[1024]{0:T(1024)S(1)} %pad_clamp_fusion), kind=kCustom, calls=%fused_computation.5 | custom fusion | bytes 16778240 | tf_op jit(solution)/shard_map/gather | solution.py:82
  141.3 20.5 %multiply_reduce_fusion.2 = f32[16,128,128]{2,1,0:T(8,128)} fusion(f32[16,16]{1,0:T(8,128)S(1)} %copy-done.9, bf16[16,16,128,128]{3,2,1,0:T(8,128)(2,1)} %param.23, bf16[16,16,128,128]{3,2,1,0:T(8,128)(2,1)} %bitcast.96), kind=kOutput, calls=%fused_computation.12 | convolution fusion | flops 2159804416 | bytes 17826816 | tf_op jit(solution)/shard_map/pnac,pndc->pnad/dot_general | solution.py:15
  161.8 8.6 %gather_fusion.3 = bf16[256,128,128]{2,1,0:T(8,128)(2,1)} fusion(bf16[32,128,128]{2,1,0:T(8,128)(2,1)S(1)} %bitcast.91, s32[1024]{0:T(1024)S(1)} %pad_clamp_fusion.2), kind=kCustom, calls=%fused_computation.3 | custom fusion | bytes 16778240 | tf_op jit(solution)/shard_map/gather | solution.py:81
  170.5 32.2 %multiply_reduce_fusion.3 = f32[16,128,128]{2,1,0:T(8,128)} fusion(f32[16,16]{1,0:T(8,128)S(1)} %copy-done.10, bf16[16,16,128,128]{3,2,1,0:T(8,128)(2,1)} %param.22, bf16[16,16,128,128]{3,2,1,0:T(8,128)(2,1)} %bitcast.97), kind=kOutput, calls=%fused_computation.13 | convolution fusion | flops 2159804416 | bytes 17826816 | tf_op jit(solution)/shard_map/pnac,pndc->pnad/dot_general | solution.py:15
  202.7 3.1 fusion.42
  205.8 1.4 gather_fusion.8
  207.2 3.5 all-to-all-start.5
  210.7 0.1 copy.65
  210.8 0.2 copy.66
  211.0 0.2 broadcast_multiply_fusion
  211.2 1.7 gather_fusion.6
  212.9 13.1 %all-to-all-done.5 = bf16[4,4,128,128]{3,2,1,0:T(8,128)(2,1)S(1)} async-done(((bf16[4,4,128,128]{3,2,1,0:T(8,128)(2,1)}), bf16[4,4,128,128]{3,2,1,0:T(8,128)(2,1)S(1)}, u32[]{:S(2)}, u32[]{:S(2)}) %all-to-all-start.5) | async-done | bytes 524320 | tf_op jit(solution)/shard_map/all_to_all | solution.py:78
  226.0 3.8 all-to-all-start.4
  229.9 0.0 all-reduce.2.cloned.1.call-start
  229.9 8.6 %gather_fusion.9 = bf16[256,128,128]{2,1,0:T(8,128)(2,1)} fusion(bf16[16,128,128]{2,1,0:T(8,128)(2,1)S(1)} %bitcast.89, s32[1024]{0:T(1024)S(1)} %pad_clamp_fusion), kind=kCustom, calls=%fused_computation.9 | custom fusion | bytes 16778240 | tf_op jit(solution)/shard_map/gather | solution.py:82
  238.6 20.5 %multiply_reduce_fusion = f32[16,128,128]{2,1,0:T(8,128)} fusion(f32[16,16]{1,0:T(8,128)S(1)} %copy-done.9, bf16[16,16,128,128]{3,2,1,0:T(8,128)(2,1)} %param.23, bf16[16,16,128,128]{3,2,1,0:T(8,128)(2,1)} %bitcast.94), kind=kOutput, calls=%fused_computation.10 | convolution fusion | flops 2159804416 | bytes 17826816 | tf_op jit(solution)/shard_map/pnac,pndc->pnad/dot_general | solution.py:15
  259.1 8.6 %gather_fusion.7 = bf16[256,128,128]{2,1,0:T(8,128)(2,1)} fusion(bf16[32,128,128]{2,1,0:T(8,128)(2,1)S(1)} %bitcast.90, s32[1024]{0:T(1024)S(1)} %pad_clamp_fusion.2), kind=kCustom, calls=%fused_computation.7 | custom fusion | bytes 16778240 | tf_op jit(solution)/shard_map/gather | solution.py:81
  267.7 20.5 %multiply_reduce_fusion.1 = f32[16,128,128]{2,1,0:T(8,128)} fusion(f32[16,16]{1,0:T(8,128)S(1)} %copy-done.10, bf16[16,16,128,128]{3,2,1,0:T(8,128)(2,1)} %param.22, bf16[16,16,128,128]{3,2,1,0:T(8,128)(2,1)} %bitcast.95), kind=kOutput, calls=%fused_computation.11 | convolution fusion | flops 2159804416 | bytes 17826816 | tf_op jit(solution)/shard_map/pnac,pndc->pnad/dot_general | solution.py:15
  288.3 2.4 divide_subtract_fusion
  290.6 0.0 copy-start.1
  290.7 1.5 fusion.39
  292.1 1.9 fusion.33
  294.0 1.3 copy.90
  295.3 1.9 fusion.43
  297.3 4.6 %fusion.16 = f32[4,4,128,128]{3,1,2,0:T(4,128)S(1)} fusion(f32[4,4,64,1]{1,2,3,0:T(8,128)S(1)} %bitcast.106, f32[8,8,128,128]{3,2,1,0:T(8,128)S(1)} %bitcast.92), kind=kOutput, calls=%fused_computation.28 | convolution fusion | flops 201326592 | bytes 5246976 | tf_op jit(solution)/shard_map/dot_general | solution.py:105
  301.8 1.0 copy.102
  302.9 0.0 all-reduce.2.cloned.1.call-update
  302.9 130.3 %all-reduce.2.cloned.1.call-done = f32[512,512]{1,0:T(8,128)} async-done(((f32[512,512]{1,0:T(8,128)}), f32[512,512]{1,0:T(8,128)}) %all-reduce.2.cloned.1.call-update) | async-done | bytes 1048592 | tf_op jit(solution)/shard_map/psum | solution.py:119
  433.3 1.4 dynamic-slice_multiply_fusion
  (30 shorter events, 0.1 us)
Async XLA Ops:
  7.2 93.1 %copy-start = (bf16[16,256,128]{2,1,0:T(8,128)(2,1)S(1)}, bf16[16,256,128]{2,1,0:T(8,128)(2,1)}, u32[]{:S(2)}) copy-start(bf16[16,256,128]{2,1,0:T(8,128)(2,1)} %param.16) | copy-start | bytes 3145732
  7.2 50.8 %all-gather.3.cloned.1.call-start = ((), (), s32[]{:S(2)}) async-start(), calls=%async_computation.6 | async-start | bytes 2621440 | tf_op jit(solution)/shard_map/all_gather | solution.py:48
  7.9 87.4 %all-gather.5.cloned.1.call-start = ((), (), s32[]{:S(2)}) async-start(), calls=%async_computation.7 | async-start | bytes 4718592 | tf_op jit(solution)/shard_map/all_gather | solution.py:49
  8.7 11.9 %all-to-all-start.2 = ((s32[1,4,4]{2,0,1:T(1,128)}), s32[1,4,4]{2,0,1:T(1,128)S(1)}, u32[]{:S(2)}, u32[]{:S(2)}) async-start(s32[1,4,4]{2,0,1:T(1,128)} %bitcast.108), calls=%async_computation.2 | async-start | bytes 4096 | tf_op jit(solution)/shard_map/all_to_all | solution.py:70
  20.5 88.7 %all-to-all-start = ((s32[1,8,4]{2,0,1:T(1,128)}), s32[1,8,4]{2,0,1:T(1,128)S(1)}, u32[]{:S(2)}, u32[]{:S(2)}) async-start(s32[1,8,4]{2,0,1:T(1,128)} %copy.53), calls=%async_computation | async-start | bytes 8192 | tf_op jit(solution)/shard_map/all_to_all | solution.py:67
  58.0 42.3 %copy-start.4 = (f32[16,128]{1,0:T(8,128)S(1)}, f32[16,128]{1,0:T(8,128)}, u32[]{:S(2)}) copy-start(f32[16,128]{1,0:T(8,128)} %param.20) | copy-start | bytes 24580
  58.0 42.3 %copy-start.8 = (f32[16]{0:T(128)S(1)}, f32[16]{0:T(128)}, u32[]{:S(2)}) copy-start(f32[16]{0:T(128)} %param.21) | copy-start | bytes 196
  100.3 13.6 %copy-start.5 = (s32[16,16]{1,0:T(8,128)S(1)}, s32[16,16]{1,0:T(8,128)}, u32[]{:S(2)}) copy-start(s32[16,16]{1,0:T(8,128)} %param.28) | copy-start | bytes 3076
  100.3 13.6 %copy-start.6 = (s32[16,16]{1,0:T(8,128)S(1)}, s32[16,16]{1,0:T(8,128)}, u32[]{:S(2)}) copy-start(s32[16,16]{1,0:T(8,128)} %param.29) | copy-start | bytes 3076
  109.2 19.5 %all-to-all-start.3 = ((bf16[4,4,128,128]{3,2,1,0:T(8,128)(2,1)}), bf16[4,4,128,128]{3,2,1,0:T(8,128)(2,1)S(1)}, u32[]{:S(2)}, u32[]{:S(2)}) async-start(bf16[4,4,128,128]{3,2,1,0:T(8,128)(2,1)} %bitcast.10), calls=%async_computation.3 | async-start | bytes 1048576 | tf_op jit(solution)/shard_map/all_to_all | solution.py:78
  128.7 33.1 %all-to-all-start.1 = ((bf16[8,4,128,128]{3,2,1,0:T(8,128)(2,1)}), bf16[8,4,128,128]{3,2,1,0:T(8,128)(2,1)S(1)}, u32[]{:S(2)}, u32[]{:S(2)}) async-start(bf16[8,4,128,128]{3,2,1,0:T(8,128)(2,1)} %bitcast.103), calls=%async_computation.1 | async-start | bytes 2097152 | tf_op jit(solution)/shard_map/all_to_all | solution.py:75
  132.7 8.6 %copy-start.9 = (f32[16,16]{1,0:T(8,128)S(1)}, f32[16,16]{1,0:T(8,128)}, u32[]{:S(2)}) copy-start(f32[16,16]{1,0:T(8,128)} %param.25) | copy-start | bytes 3076
  161.8 8.6 %copy-start.10 = (f32[16,16]{1,0:T(8,128)S(1)}, f32[16,16]{1,0:T(8,128)}, u32[]{:S(2)}) copy-start(f32[16,16]{1,0:T(8,128)} %param.24) | copy-start | bytes 3076
  170.5 32.2 %copy-start.2 = (f32[16,128,128]{2,1,0:T(8,128)S(1)}, f32[16,128,128]{2,1,0:T(8,128)}, u32[]{:S(2)}) copy-start(f32[16,128,128]{2,1,0:T(8,128)} %get-tuple-element.7) | copy-start | bytes 3145732
  170.5 40.2 %copy-start.7 = (s32[16,2]{0,1:T(2,128)S(1)}, s32[16,2]{0,1:T(2,128)}, u32[]{:S(2)}) copy-start(s32[16,2]{0,1:T(2,128)} %param.17) | copy-start | bytes 388
  207.2 18.8 %all-to-all-start.5 = ((bf16[4,4,128,128]{3,2,1,0:T(8,128)(2,1)}), bf16[4,4,128,128]{3,2,1,0:T(8,128)(2,1)S(1)}, u32[]{:S(2)}, u32[]{:S(2)}) async-start(bf16[4,4,128,128]{3,2,1,0:T(8,128)(2,1)} %bitcast.16), calls=%async_computation.5 | async-start | bytes 1048576 | tf_op jit(solution)/shard_map/all_to_all | solution.py:78
  226.0 33.0 %all-to-all-start.4 = ((bf16[8,4,128,128]{3,2,1,0:T(8,128)(2,1)}), bf16[8,4,128,128]{3,2,1,0:T(8,128)(2,1)S(1)}, u32[]{:S(2)}, u32[]{:S(2)}) async-start(bf16[8,4,128,128]{3,2,1,0:T(8,128)(2,1)} %bitcast.102), calls=%async_computation.4 | async-start | bytes 2097152 | tf_op jit(solution)/shard_map/all_to_all | solution.py:75
  229.9 203.4 %all-reduce.2.cloned.1.call-start = ((), (), s32[]{:S(2)}) async-start(), calls=%async_computation.8 | async-start | bytes 2097152 | tf_op jit(solution)/shard_map/psum | solution.py:119
  267.7 20.5 %copy-start.3 = (f32[16,128,128]{2,1,0:T(8,128)S(1)}, f32[16,128,128]{2,1,0:T(8,128)}, u32[]{:S(2)}) copy-start(f32[16,128,128]{2,1,0:T(8,128)} %get-tuple-element.7) | copy-start | bytes 3145732
  290.6 11.2 %copy-start.1 = (f32[16,128,128]{2,1,0:T(8,128)}, f32[16,128,128]{2,1,0:T(8,128)S(1)}, u32[]{:S(2)}) copy-start(f32[16,128,128]{2,1,0:T(8,128)S(1)} %divide_subtract_fusion) | copy-start | bytes 3145732
Sparse Core Ops, SparseCore 0:
  9.6 48.3 all-gather.2
  59.9 35.3 all-gather.4
  303.0 130.1 all-reduce.1
where the time goes:
time: 446 us; the launch traced here: 441 us
  waiting for transfers between devices  227 us (51%)
  matrix products  111 us (25%)
  local copies, waits for them, and re-layouts  55 us (12%)
  starting transfers between devices  26 us (6%)
  between operations  14.2 us (3%)
  other arithmetic  8.5 us (2%)
    psum x1, waiting for transfers between devices, body(): summed = lax.psum(partial_sum, ('ia', 'ja'))  130 us
    dot_general x4, matrix products, coupled(): jnp.einsum('pnac,pndc->pnad', left_side, margin_blocks, preferred_element...  93.8 us
    all_gather x1, waiting for transfers between devices, body(): row_slabs = lax.all_gather(slabs, 'ja', axis=0, tiled=True)  33.6 us
    all_gather x1, waiting for transfers between devices, body(): col_slabs = lax.all_gather(slabs, 'ia', axis=0, tiled=True)  32.9 us
    all_to_all x2, waiting for transfers between devices, body(): lax.all_to_all(sent[asked_cols], 'ja', split_axis=0, concat_axis=0, tiled...  25.9 us
    gather x2, local copies, waits for them, and re-layouts, body(): near_rows = table_rows[link_i]  17.3 us
    gather x2, local copies, waits for them, and re-layouts, body(): near_cols = table_cols[link_j]  17.3 us
  transfers between devices with their start and end apart: 9, of which 6 were waited for; matrix products, arithmetic and copies ran while one was open for 19% of the time, Pallas kernels for 0%

commit v1 on v0

--- a/solution.py
+++ b/solution.py
@@ -1,3 +1,4 @@
+import functools
 import math
 import jax
 import jax.numpy as jnp
@@ -6,6 +7,22 @@
 
 BLK = 128
 ITERS = 2
+
+
+def local_data_finish(piece_in, axis_id):
+    world = lax.axis_size(axis_id)
+    near = piece_in
+    crops = [near]
+    v_next = [(dev - 1, dev) for dev in range(1, world)] + [(world - 1, 0)]
+    for _ in range(world - 1):
+        near = lax.ppermute(near, axis_id, v_next)
+        crops += [near]
+    fresh = jnp.concatenate([*reversed(crops)], 0)
+    spare = jnp.roll(fresh, (lax.axis_index(axis_id) + 1) * near.shape[0], 0)
+    return spare
+
+
+_extend_classes = functools.partial(local_data_finish, axis_id="ja")
 
 
 def coupled(near_blocks, margin_blocks, weights):
@@ -45,7 +62,7 @@
     col_peers = lax.axis_size("ja")
     row_slots = ask_i.shape[2]
     col_slots = ask_j.shape[2]
-    row_slabs = lax.all_gather(slabs, "ja", axis=0, tiled=True)
+    row_slabs = _extend_classes(slabs)
     col_slabs = lax.all_gather(slabs, "ia", axis=0, tiled=True)
     rows_first = row_slabs.reshape(-1, BLK, aux_count)[
         pair_first[:, None] * block_count + dom_blocks

time: 446 us -> 408 us (0.915)
  waiting for transfers between devices: 227 us -> 187 us
    all_gather x1 -> x0, waiting for transfers between devices: 33.6 us -> none  [body(): row_slabs = lax.all_gather(slabs, 'ja', axis=0, tiled=True)]
    all_gather x1, waiting for transfers between devices: 32.9 us -> 0.01 us  [body(): col_slabs = lax.all_gather(slabs, 'ia', axis=0, tiled=True)]
    ppermute x0 -> x3, waiting for transfers between devices: none -> 27.6 us  [local_data_finish(): near = lax.ppermute(near, axis_id, v_next)]
    all_to_all x1, waiting for transfers between devices: 0.01 us -> 4.61 us  [body(): lax.all_to_all(ask_i, 'ia', split_axis=1, concat_axis=0, tiled=True)]
  transfers between devices with their start and end apart: 9 -> 11, of which waited for: 6 -> 7; matrix products, arithmetic and copies ran while one was open for 19% -> 18% of each run, Pallas kernels for 0% -> 0%
where the time goes in v1:
time: 408 us; the launch traced here: 402 us
  waiting for transfers between devices  187 us (46%)
  matrix products  111 us (27%)
  local copies, waits for them, and re-layouts  55.9 us (14%)
  starting transfers between devices  25.3 us (6%)
  between operations  14.5 us (4%)
  other arithmetic  8.5 us (2%)
    psum x1, waiting for transfers between devices, body(): summed = lax.psum(partial_sum, ('ia', 'ja'))  130 us
    dot_general x4, matrix products, coupled(): jnp.einsum('pnac,pndc->pnad', left_side, margin_blocks, preferred_element...  93.8 us
    ppermute x3, waiting for transfers between devices, local_data_finish(): near = lax.ppermute(near, axis_id, v_next)  27.6 us
    all_to_all x2, waiting for transfers between devices, body(): lax.all_to_all(sent[asked_cols], 'ja', split_axis=0, concat_axis=0, tiled...  23.7 us
    gather x2, local copies, waits for them, and re-layouts, body(): near_rows = table_rows[link_i]  17.3 us
    gather x2, local copies, waits for them, and re-layouts, body(): near_cols = table_cols[link_j]  17.3 us
  transfers between devices with their start and end apart: 11, of which 7 were waited for; matrix products, arithmetic and copies ran while one was open for 18% of the time, Pallas kernels for 0%

profile of v1, /device:TPU:0, one launch (start us, length us, event | category | flops | bytes accessed | tf_op | source)
XLA Modules:
  0.0 402.4 jit_solution(10152657278322399962)
XLA Ops:
  7.2 0.0 copy-start
  7.2 0.0 all-gather.2.cloned.1.call-start
  7.2 0.7 all-gather.2.cloned.1.call-update
  7.9 3.1 collective-permute-start
  11.0 3.9 all-to-all-start.2
  14.9 10.3 %collective-permute-done = bf16[1,512,512]{2,1,0:T(8,128)(2,1)S(1)} collective-permute-done((bf16[1,512,512]{2,1,0:T(8,128)(2,1)}, bf16[1,512,512]{2,1,0:T(8,128)(2,1)S(1)}, u32[]{:S(2)}, u32[]{:S(2)}) %collective-permute-start) | collective-permute-done | bytes 524320 | tf_op jit(solution)/shard_map/ppermute | solution.py:18
  25.2 0.7 broadcast_multiply_fusion.1
  25.9 0.7 compare_select_fusion.5
  26.6 0.1 copy.48
  26.7 0.1 reshape.141
  26.8 0.1 copy.50
  26.8 0.1 reshape.149
  26.9 1.4 copy.53
  28.3 11.8 %collective-permute-done.1 = bf16[1,512,512]{2,1,0:T(8,128)(2,1)S(1)} collective-permute-done((bf16[1,512,512]{2,1,0:T(8,128)(2,1)S(1)}, bf16[1,512,512]{2,1,0:T(8,128)(2,1)S(1)}, u32[]{:S(2)}, u32[]{:S(2)}) %collective-permute-start.1) | collective-permute-done | bytes 524320 | tf_op jit(solution)/shard_map/ppermute | solution.py:18
  40.1 3.5 all-to-all-start
  43.6 0.1 reshape.173
  43.7 4.6 %all-to-all-done = s32[1,8,4]{2,0,1:T(1,128)S(1)} async-done(((s32[1,8,4]{2,0,1:T(1,128)}), s32[1,8,4]{2,0,1:T(1,128)S(1)}, u32[]{:S(2)}, u32[]{:S(2)}) %all-to-all-start) | async-done | bytes 160 | tf_op jit(solution)/shard_map/all_to_all | solution.py:84
  48.3 0.1 copy.54
  48.4 0.1 copy.55
  48.5 0.1 reshape.157
  48.5 5.5 %collective-permute-done.2 = bf16[1,512,512]{2,1,0:T(8,128)(2,1)S(1)} collective-permute-done((bf16[1,512,512]{2,1,0:T(8,128)(2,1)S(1)}, bf16[1,512,512]{2,1,0:T(8,128)(2,1)S(1)}, u32[]{:S(2)}, u32[]{:S(2)}) %collective-permute-start.2) | collective-permute-done | bytes 524320 | tf_op jit(solution)/shard_map/ppermute | solution.py:18
  54.2 1.1 constant_dynamic-update-slice_fusion.4
  55.4 1.1 constant_dynamic-update-slice_fusion
  56.5 0.1 constant_dynamic-slice_fusion
  56.6 0.0 copy-start.4
  56.7 2.8 gather_fusion
  59.5 5.0 %gather_fusion.1 = bf16[32,128,512]{2,1,0:T(8,128)(2,1)} fusion(bf16[32,128,512]{2,1,0:T(8,128)(2,1)} %bitcast.98, s32[1024]{0:T(1024)S(1)} %pad_clamp_fusion.4), kind=kCustom, calls=%fused_computation.1 | custom fusion | bytes 8388736 | tf_op jit(solution)/shard_map/gather | solution.py:70
  64.5 0.0 copy-start.5
  64.5 7.5 %fusion.36 = (bf16[16,128,128]{2,1,0:T(8,128)(2,1)S(1)}, f32[16,128,128]{2,1,0:T(8,128)}) fusion(f32[16]{0:T(128)S(1)} %copy-done.8, f32[16,128]{1,0:T(8,128)S(1)} %copy-done.4, bf16[16,256,512]{2,1,0:T(8,128)(2,1)} %bitcast.100, bf16[16,256,128]{2,1,0:T(8,128)(2,1)S(1)} %copy-done, bf16[16,256,512]{2,1,0:T(8,128)(2,1)} %bitcast.99), kind=kOutput, calls=%fused_computation.44 | convolution fusion | flops 1345585152 | bytes 11018304 | tf_op jit(solution)/shard_map/paq,pbq->pab/dot_general | solution.py:79
  72.0 1.4 gather_fusion.4
  73.4 3.5 all-to-all-start.3
  76.9 0.1 reshape.165
  77.0 0.1 reshape.181
  77.1 1.7 gather_fusion.2
  78.8 10.5 %all-to-all-done.3 = bf16[4,4,128,128]{3,2,1,0:T(8,128)(2,1)S(1)} async-done(((bf16[4,4,128,128]{3,2,1,0:T(8,128)(2,1)}), bf16[4,4,128,128]{3,2,1,0:T(8,128)(2,1)S(1)}, u32[]{:S(2)}, u32[]{:S(2)}) %all-to-all-start.3) | async-done | bytes 524320 | tf_op jit(solution)/shard_map/all_to_all | solution.py:95
  89.3 3.9 all-to-all-start.1
  93.3 8.6 %gather_fusion.5 = bf16[256,128,128]{2,1,0:T(8,128)(2,1)} fusion(bf16[16,128,128]{2,1,0:T(8,128)(2,1)S(1)} %bitcast.88, s32[1024]{0:T(1024)S(1)} %pad_clamp_fusion), kind=kCustom, calls=%fused_computation.5 | custom fusion | bytes 16778240 | tf_op jit(solution)/shard_map/gather | solution.py:99
  101.9 20.5 %multiply_reduce_fusion.2 = f32[16,128,128]{2,1,0:T(8,128)} fusion(f32[16,16]{1,0:T(8,128)S(1)} %copy-done.9, bf16[16,16,128,128]{3,2,1,0:T(8,128)(2,1)} %param.23, bf16[16,16,128,128]{3,2,1,0:T(8,128)(2,1)} %bitcast.96), kind=kOutput, calls=%fused_computation.12 | convolution fusion | flops 2159804416 | bytes 17826816 | tf_op jit(solution)/shard_map/pnac,pndc->pnad/dot_general | solution.py:32
  122.4 8.6 %gather_fusion.3 = bf16[256,128,128]{2,1,0:T(8,128)(2,1)} fusion(bf16[32,128,128]{2,1,0:T(8,128)(2,1)S(1)} %bitcast.91, s32[1024]{0:T(1024)S(1)} %pad_clamp_fusion.2), kind=kCustom, calls=%fused_computation.3 | custom fusion | bytes 16778240 | tf_op jit(solution)/shard_map/gather | solution.py:98
  131.1 32.2 %multiply_reduce_fusion.3 = f32[16,128,128]{2,1,0:T(8,128)} fusion(f32[16,16]{1,0:T(8,128)S(1)} %copy-done.10, bf16[16,16,128,128]{3,2,1,0:T(8,128)(2,1)} %param.22, bf16[16,16,128,128]{3,2,1,0:T(8,128)(2,1)} %bitcast.97), kind=kOutput, calls=%fused_computation.13 | convolution fusion | flops 2159804416 | bytes 17826816 | tf_op jit(solution)/shard_map/pnac,pndc->pnad/dot_general | solution.py:32
  163.3 3.1 fusion.42
  166.4 1.4 gather_fusion.8
  167.9 3.5 all-to-all-start.5
  171.3 0.1 copy.65
  171.4 0.2 copy.66
  171.6 0.2 broadcast_multiply_fusion
  171.8 1.7 gather_fusion.6
  173.5 13.1 %all-to-all-done.5 = bf16[4,4,128,128]{3,2,1,0:T(8,128)(2,1)S(1)} async-done(((bf16[4,4,128,128]{3,2,1,0:T(8,128)(2,1)}), bf16[4,4,128,128]{3,2,1,0:T(8,128)(2,1)S(1)}, u32[]{:S(2)}, u32[]{:S(2)}) %all-to-all-start.5) | async-done | bytes 524320 | tf_op jit(solution)/shard_map/all_to_all | solution.py:95
  186.7 3.9 all-to-all-start.4
  190.5 0.0 all-reduce.2.cloned.1.call-start
  190.6 8.6 %gather_fusion.9 = bf16[256,128,128]{2,1,0:T(8,128)(2,1)} fusion(bf16[16,128,128]{2,1,0:T(8,128)(2,1)S(1)} %bitcast.89, s32[1024]{0:T(1024)S(1)} %pad_clamp_fusion), kind=kCustom, calls=%fused_computation.9 | custom fusion | bytes 16778240 | tf_op jit(solution)/shard_map/gather | solution.py:99
  199.2 20.5 %multiply_reduce_fusion = f32[16,128,128]{2,1,0:T(8,128)} fusion(f32[16,16]{1,0:T(8,128)S(1)} %copy-done.9, bf16[16,16,128,128]{3,2,1,0:T(8,128)(2,1)} %param.23, bf16[16,16,128,128]{3,2,1,0:T(8,128)(2,1)} %bitcast.94), kind=kOutput, calls=%fused_computation.10 | convolution fusion | flops 2159804416 | bytes 17826816 | tf_op jit(solution)/shard_map/pnac,pndc->pnad/dot_general | solution.py:32
  219.7 8.6 %gather_fusion.7 = bf16[256,128,128]{2,1,0:T(8,128)(2,1)} fusion(bf16[32,128,128]{2,1,0:T(8,128)(2,1)S(1)} %bitcast.90, s32[1024]{0:T(1024)S(1)} %pad_clamp_fusion.2), kind=kCustom, calls=%fused_computation.7 | custom fusion | bytes 16778240 | tf_op jit(solution)/shard_map/gather | solution.py:98
  228.4 20.5 %multiply_reduce_fusion.1 = f32[16,128,128]{2,1,0:T(8,128)} fusion(f32[16,16]{1,0:T(8,128)S(1)} %copy-done.10, bf16[16,16,128,128]{3,2,1,0:T(8,128)(2,1)} %param.22, bf16[16,16,128,128]{3,2,1,0:T(8,128)(2,1)} %bitcast.95), kind=kOutput, calls=%fused_computation.11 | convolution fusion | flops 2159804416 | bytes 17826816 | tf_op jit(solution)/shard_map/pnac,pndc->pnad/dot_general | solution.py:32
  248.9 2.4 divide_subtract_fusion
  251.3 1.5 fusion.39
  252.8 1.9 fusion.33
  254.7 1.3 copy.90
  256.0 1.9 fusion.43
  257.9 4.6 %fusion.16 = f32[4,4,128,128]{3,1,2,0:T(4,128)S(1)} fusion(f32[4,4,64,1]{1,2,3,0:T(8,128)S(1)} %bitcast.106, f32[8,8,128,128]{3,2,1,0:T(8,128)S(1)} %bitcast.93), kind=kOutput, calls=%fused_computation.28 | convolution fusion | flops 201326592 | bytes 5246976 | tf_op jit(solution)/shard_map/dot_general | solution.py:122
  262.5 1.0 copy.102
  263.5 0.0 all-reduce.2.cloned.1.call-update
  263.6 130.3 %all-reduce.2.cloned.1.call-done = f32[512,512]{1,0:T(8,128)} async-done(((f32[512,512]{1,0:T(8,128)}), f32[512,512]{1,0:T(8,128)}) %all-reduce.2.cloned.1.call-update) | async-done | bytes 1048592 | tf_op jit(solution)/shard_map/psum | solution.py:136
  393.9 1.4 dynamic-slice_multiply_fusion
  (41 shorter events, 0.3 us)
Async XLA Ops:
  7.2 57.3 %copy-start = (bf16[16,256,128]{2,1,0:T(8,128)(2,1)S(1)}, bf16[16,256,128]{2,1,0:T(8,128)(2,1)}, u32[]{:S(2)}) copy-start(bf16[16,256,128]{2,1,0:T(8,128)(2,1)} %param.16) | copy-start | bytes 3145732
  7.2 52.3 %all-gather.2.cloned.1.call-start = ((), (), s32[]{:S(2)}) async-start(), calls=%async_computation.6 | async-start | bytes 4718592 | tf_op jit(solution)/shard_map/all_gather | solution.py:66
  7.9 17.3 %collective-permute-start = (bf16[1,512,512]{2,1,0:T(8,128)(2,1)}, bf16[1,512,512]{2,1,0:T(8,128)(2,1)S(1)}, u32[]{:S(2)}, u32[]{:S(2)}) collective-permute-start(bf16[1,512,512]{2,1,0:T(8,128)(2,1)} %param.15), channel_id=1, source_target_pairs={{0,1},{1,2},{2,3},{3,0},{4,5},{5,6},{6,7},{7,4},{8,9},{9,10},{10,1... | collective-permute-start | bytes 1572872 | tf_op jit(solution)/shard_map/ppermute | solution.py:18
  11.0 29.1 %all-to-all-start.2 = ((s32[1,4,4]{2,0,1:T(1,128)}), s32[1,4,4]{2,0,1:T(1,128)S(1)}, u32[]{:S(2)}, u32[]{:S(2)}) async-start(s32[1,4,4]{2,0,1:T(1,128)} %bitcast.108), calls=%async_computation.2 | async-start | bytes 4096 | tf_op jit(solution)/shard_map/all_to_all | solution.py:87
  25.2 14.9 %collective-permute-start.1 = (bf16[1,512,512]{2,1,0:T(8,128)(2,1)S(1)}, bf16[1,512,512]{2,1,0:T(8,128)(2,1)S(1)}, u32[]{:S(2)}, u32[]{:S(2)}) collective-permute-start(bf16[1,512,512]{2,1,0:T(8,128)(2,1)S(1)} %collective-permute-done), channel_id=1, source_target_pairs={{0,1},{1,2},{2,3},{3,0},{4,5},{5,6},{6,7},{7,4},{8,9},{9,10},{10,1... | collective-permute-start | bytes 1572872 | tf_op jit(solution)/shard_map/ppermute | solution.py:18
  40.1 14.0 %collective-permute-start.2 = (bf16[1,512,512]{2,1,0:T(8,128)(2,1)S(1)}, bf16[1,512,512]{2,1,0:T(8,128)(2,1)S(1)}, u32[]{:S(2)}, u32[]{:S(2)}) collective-permute-start(bf16[1,512,512]{2,1,0:T(8,128)(2,1)S(1)} %collective-permute-done.1), channel_id=1, source_target_pairs={{0,1},{1,2},{2,3},{3,0},{4,5},{5,6},{6,7},{7,4},{8,9},{9,10},{10,1... | collective-permute-start | bytes 1572872 | tf_op jit(solution)/shard_map/ppermute | solution.py:18
  40.1 8.2 %all-to-all-start = ((s32[1,8,4]{2,0,1:T(1,128)}), s32[1,8,4]{2,0,1:T(1,128)S(1)}, u32[]{:S(2)}, u32[]{:S(2)}) async-start(s32[1,8,4]{2,0,1:T(1,128)} %copy.53), calls=%async_computation | async-start | bytes 8192 | tf_op jit(solution)/shard_map/all_to_all | solution.py:84
  56.6 7.8 %copy-start.4 = (f32[16,128]{1,0:T(8,128)S(1)}, f32[16,128]{1,0:T(8,128)}, u32[]{:S(2)}) copy-start(f32[16,128]{1,0:T(8,128)} %param.20) | copy-start | bytes 24580
  56.7 7.8 %copy-start.8 = (f32[16]{0:T(128)S(1)}, f32[16]{0:T(128)}, u32[]{:S(2)}) copy-start(f32[16]{0:T(128)} %param.21) | copy-start | bytes 196
  64.5 12.4 %copy-start.5 = (s32[16,16]{1,0:T(8,128)S(1)}, s32[16,16]{1,0:T(8,128)}, u32[]{:S(2)}) copy-start(s32[16,16]{1,0:T(8,128)} %param.28) | copy-start | bytes 3076
  64.5 12.5 %copy-start.6 = (s32[16,16]{1,0:T(8,128)S(1)}, s32[16,16]{1,0:T(8,128)}, u32[]{:S(2)}) copy-start(s32[16,16]{1,0:T(8,128)} %param.29) | copy-start | bytes 3076
  73.4 15.9 %all-to-all-start.3 = ((bf16[4,4,128,128]{3,2,1,0:T(8,128)(2,1)}), bf16[4,4,128,128]{3,2,1,0:T(8,128)(2,1)S(1)}, u32[]{:S(2)}, u32[]{:S(2)}) async-start(bf16[4,4,128,128]{3,2,1,0:T(8,128)(2,1)} %bitcast.10), calls=%async_computation.3 | async-start | bytes 1048576 | tf_op jit(solution)/shard_map/all_to_all | solution.py:95
  89.3 33.1 %all-to-all-start.1 = ((bf16[8,4,128,128]{3,2,1,0:T(8,128)(2,1)}), bf16[8,4,128,128]{3,2,1,0:T(8,128)(2,1)S(1)}, u32[]{:S(2)}, u32[]{:S(2)}) async-start(bf16[8,4,128,128]{3,2,1,0:T(8,128)(2,1)} %bitcast.103), calls=%async_computation.1 | async-start | bytes 2097152 | tf_op jit(solution)/shard_map/all_to_all | solution.py:92
  93.3 8.7 %copy-start.9 = (f32[16,16]{1,0:T(8,128)S(1)}, f32[16,16]{1,0:T(8,128)}, u32[]{:S(2)}) copy-start(f32[16,16]{1,0:T(8,128)} %param.25) | copy-start | bytes 3076
  122.4 8.6 %copy-start.10 = (f32[16,16]{1,0:T(8,128)S(1)}, f32[16,16]{1,0:T(8,128)}, u32[]{:S(2)}) copy-start(f32[16,16]{1,0:T(8,128)} %param.24) | copy-start | bytes 3076
  131.1 32.2 %copy-start.2 = (f32[16,128,128]{2,1,0:T(8,128)S(1)}, f32[16,128,128]{2,1,0:T(8,128)}, u32[]{:S(2)}) copy-start(f32[16,128,128]{2,1,0:T(8,128)} %get-tuple-element.7) | copy-start | bytes 3145732
  131.1 40.3 %copy-start.7 = (s32[16,2]{0,1:T(2,128)S(1)}, s32[16,2]{0,1:T(2,128)}, u32[]{:S(2)}) copy-start(s32[16,2]{0,1:T(2,128)} %param.17) | copy-start | bytes 388
  167.9 18.8 %all-to-all-start.5 = ((bf16[4,4,128,128]{3,2,1,0:T(8,128)(2,1)}), bf16[4,4,128,128]{3,2,1,0:T(8,128)(2,1)S(1)}, u32[]{:S(2)}, u32[]{:S(2)}) async-start(bf16[4,4,128,128]{3,2,1,0:T(8,128)(2,1)} %bitcast.16), calls=%async_computation.5 | async-start | bytes 1048576 | tf_op jit(solution)/shard_map/all_to_all | solution.py:95
  186.7 33.1 %all-to-all-start.4 = ((bf16[8,4,128,128]{3,2,1,0:T(8,128)(2,1)}), bf16[8,4,128,128]{3,2,1,0:T(8,128)(2,1)S(1)}, u32[]{:S(2)}, u32[]{:S(2)}) async-start(bf16[8,4,128,128]{3,2,1,0:T(8,128)(2,1)} %bitcast.102), calls=%async_computation.4 | async-start | bytes 2097152 | tf_op jit(solution)/shard_map/all_to_all | solution.py:92
  190.5 203.4 %all-reduce.2.cloned.1.call-start = ((), (), s32[]{:S(2)}) async-start(), calls=%async_computation.7 | async-start | bytes 2097152 | tf_op jit(solution)/shard_map/psum | solution.py:136
  228.4 20.5 %copy-start.3 = (f32[16,128,128]{2,1,0:T(8,128)S(1)}, f32[16,128,128]{2,1,0:T(8,128)}, u32[]{:S(2)}) copy-start(f32[16,128,128]{2,1,0:T(8,128)} %get-tuple-element.7) | copy-start | bytes 3145732
  251.3 11.2 %copy-start.1 = (f32[16,128,128]{2,1,0:T(8,128)}, f32[16,128,128]{2,1,0:T(8,128)S(1)}, u32[]{:S(2)}) copy-start(f32[16,128,128]{2,1,0:T(8,128)S(1)} %divide_subtract_fusion) | copy-start | bytes 3145732
Sparse Core Ops, SparseCore 0:
  9.9 39.3 all-gather.1
  263.7 130.1 all-reduce.1
